TPU v7x, 128 devices: a whole 4x4x4 slice. The times are simulated.
128 devices in a mesh: tier: 8 (over y, z_lo), tile: 16 (over x, z_hi, core).
Axes of the slice: x: 4, y: 4, z: 4 (z_hi: 2, z_lo: 2; z = z_hi * 2 + z_lo), core: 2. Of those that a mesh axis runs over, the one named last changes fastest.
Arguments:
- warming_above_ambient: float32 [8, 16, 512, 2048], P('tier', None, 'tile'), may hold values from -6 to 6
- substance_label: int32 [8, 16, 512, 2048], P('tier', None, 'tile'), may hold values from 0 to 15
- glue_zone_label: int32 [512, 2048], P('tile'), may hold values from 0 to 7
- patch_label_per_cell: int32 [8, 512, 2048], P('tier', 'tile'), may hold values from 0 to 127
- heat_conductance_per_substance: float32 [16], replicated, may hold values from 0.3 to 4
- dissipation_per_patch: float32 [8, 128], P('tier'), may hold values from 0.5 to 5
- glue_sheet_reciprocal_operators: float32 [8, 16, 16], replicated, may hold values from -0.3 to 1.3, as said below
Outputs:
- final_state: float32 [8, 16, 512, 2048], P('tier', None, 'tile')
Inputs may be any that keep to these rules, and one draw needn't show every extreme that they name: `glue_sheet_reciprocal_operators`: each matrix has diagonal entries of 0.6 to 1.0 plus a perturbation, and perturbed entries elsewhere.
All inputs are finite; a program needn't handle non-finite values.
Results may differ from a plain program's by a relative error of at most 0.0001.
Values sent between devices are 32-bit elements; how exact they have to be, the bound alone decides.
A program may use at most 128 MiB of HBM per device.

v0:
```python
import jax
import jax.numpy as jnp
from jax import lax
from jax.sharding import PartitionSpec as P

MATERIALS = 16
REGIONS = 8
POWER_TILES = 128
STEPS = 2


step_dt = 0.04


def padded(cells, sides, width):
    for axis, dim in sides:
        count = lax.axis_size(axis)
        ends = count - 1
        head = lax.slice_in_dim(cells, 0, width, axis=dim)
        tail = lax.slice_in_dim(cells, cells.shape[dim] - width, cells.shape[dim], axis=dim)
        cells = jnp.concatenate(
            [
                lax.ppermute(tail, axis, [(i, (i + 1) % count) for i in range(ends)]),
                cells,
                lax.ppermute(head, axis, [((i + 1) % count, i) for i in range(ends)]),
            ],
            axis=dim,
        )
    return cells


def pad_axis(field, axis, low, high):
    widths = [(0, 0)] * field.ndim
    widths[axis] = (low, high)
    return jnp.pad(field, widths)


def conduct(padded_t, padded_k):
    centre = padded_t[..., 1:-1, :]
    kcell = padded_k[..., 1:-1, :]
    flux = 0.5 * (kcell + padded_k[..., 2:, :]) * (padded_t[..., 2:, :] - centre)
    flux = flux + 0.5 * (kcell + padded_k[..., :-2, :]) * (padded_t[..., :-2, :] - centre)
    side_t = pad_axis(centre, centre.ndim - 1, 1, 1)
    side_k = pad_axis(kcell, kcell.ndim - 1, 1, 1)
    flux = flux + 0.5 * (kcell + side_k[..., 2:]) * (side_t[..., 2:] - centre)
    flux = flux + 0.5 * (kcell + side_k[..., :-2]) * (side_t[..., :-2] - centre)
    face = (
        0.5
        * (kcell[..., 1:, :, :] + kcell[..., :-1, :, :])
        * (centre[..., 1:, :, :] - centre[..., :-1, :, :])
    )
    axis = centre.ndim - 3
    return flux + pad_axis(face, axis, 0, 1) - pad_axis(face, axis, 1, 0)


def select_solve(matrices, planes, regions):
    solved = jnp.zeros((matrices.shape[1],) + planes.shape[1:], jnp.float32)
    for which in range(REGIONS):
        mapped = jnp.einsum("ij,jxc->ixc", matrices[which], planes, precision=lax.Precision.HIGHEST)
        solved = solved + jnp.where(regions == which, mapped, 0.0)
    return solved


def local(
    warming_above_ambient,
    substance_label,
    glue_zone_label,
    patch_label_per_cell,
    heat_conductance_per_substance,
    dissipation_per_patch,
    glue_sheet_reciprocal_operators,
):
    kappa = jnp.zeros(substance_label.shape, jnp.float32)
    for which in range(MATERIALS):
        kappa = jnp.where(substance_label == which, heat_conductance_per_substance[which], kappa)
    onehot = (patch_label_per_cell[0][..., None] == lax.iota(jnp.int32, POWER_TILES)).astype(
        jnp.float32
    )
    source = jnp.dot(
        onehot.reshape(-1, POWER_TILES), dissipation_per_patch[0], precision=lax.Precision.HIGHEST
    )
    source = source.reshape(patch_label_per_cell.shape[1:])
    tier_index = lax.axis_index("tier")
    heating_snapshot = warming_above_ambient
    for step in range(STEPS):
        joined = padded(jnp.stack([heating_snapshot, kappa]), (("tile", 3),), 1)
        padded_t = joined[0]
        padded_k = joined[1]
        heating_snapshot = heating_snapshot + step_dt * conduct(padded_t, padded_k)
        heating_snapshot = heating_snapshot.at[:, 0].add(step_dt * source)
        planes = jnp.stack([heating_snapshot[0, 0], heating_snapshot[0, -1]])
        gathered = lax.all_gather(planes, "tier", axis=0, tiled=True)
        own_rows = lax.dynamic_slice_in_dim(glue_sheet_reciprocal_operators, 2 * tier_index, 2, 1)
        updated = select_solve(own_rows, gathered, glue_zone_label)
        heating_snapshot = heating_snapshot.at[0, 0].set(updated[0]).at[0, -1].set(updated[1])
    return heating_snapshot


def solution(mesh):
    in_specs = (
        P("tier", None, "tile", None),
        P("tier", None, "tile", None),
        P("tile", None),
        P("tier", "tile", None),
        P(),
        P("tier", None),
        P(),
    )
    out_specs = P("tier", None, "tile", None)
    return jax.shard_map(local, mesh=mesh, in_specs=in_specs, out_specs=out_specs, check_vma=False)
```

profile of v0, /device:TPU:7, one launch (start us, length us, event | category | flops | bytes accessed | tf_op | source)
XLA Modules:
  0.0 561.8 jit_solution(4008973471089859055)
XLA Ops:
  8.5 5.0 stack.22
  13.5 44.8 %fusion.8 = f32[1,1,16,32,2048]{4,0,3,2,1:T(1,128)S(1)} fusion(s32[1,16,32,2048]{3,2,1,0:T(8,128)S(1)} %copy-done.16, f32[]{:T(128)} %bitcast.15, f32[]{:T(128)} %bitcast.14, f32[]{:T(128)} %bitcast.13, f32[]{:T(128)} %bitcast.12, f32[]{:T(128)} %bitcast.11, f32[]{:T(128)} %bitcast.10, f32[]{:T(128)} %bitcast.9, f32[]{:T(128)} %bitcast.8, f32[]{:T(128)} %bitcast.7, ...), kind=kLoop, calls=%fused_computation.33 | loop fusion | flops 33554432 | bytes 8388672 | tf_op jit(solution)/shard_map/stack | solution.py:86
  58.9 6.1 %collective-permute-start = (f32[2,1,16,1,2048]{4,0,3,2,1:T(2,128)S(1)}, f32[2,1,16,1,2048]{4,0,3,2,1:T(2,128)S(1)}, u32[]{:S(2)}, u32[]{:S(2)}) collective-permute-start(f32[2,1,16,1,2048]{4,0,3,2,1:T(2,128)S(1)} %get-tuple-element.77), channel_id=1, source_target_pairs={{0,1},{1,2},{2,3},{3,4},{4,5},{5,6},{6,7},{7,8},{8,9},{9,10},{10,1... | collective-permute-start | bytes 786440 | tf_op jit(solution)/shard_map/ppermute | solution.py:23
  67.1 23.6 %fusion.1 = f32[1,32,2048]{2,0,1:T(1,128)S(1)} fusion(s32[32,2048]{1,0:T(8,128)S(1)} %bitcast.110, f32[1,128]{1,0:T(1,128)S(1)} %copy-done.20), kind=kOutput, calls=%fused_computation.2 | convolution fusion | flops 109051904 | bytes 524800 | tf_op jit(solution)/shard_map/dot_general | solution.py:79
  90.8 8.0 %fusion.5 = f32[2,1,16,34,2048]{4,0,3,2,1:T(2,128)S(1)} fusion(f32[1,1,16,32,2048]{4,0,3,2,1:T(1,128)S(1)} %fusion.8, f32[2,1,16,1,2048]{4,0,3,2,1:T(2,128)S(1)} %collective-permute-done.1, f32[1,1,16,32,2048]{4,0,3,2,1:T(1,128)S(1)} %stack.22, f32[2,1,16,1,2048]{4,0,3,2,1:T(2,128)S(1)} %collective-permute-done), kind=kLoop, calls=%fused_computation.23 | loop fusion | flops 6684672 | bytes 17825792 | tf_op jit(solution)/shard_map/concatenate | solution.py:21
  98.8 7.9 %slice_bitcast_fusion.3 = (f32[1,16,34,2048]{3,0,2,1:T(1,128)S(1)}, f32[1,16,34,2048]{3,0,2,1:T(1,128)}) fusion(f32[2,1,16,34,2048]{4,0,3,2,1:T(2,128)S(1)} %fusion.5), kind=kLoop, calls=%fused_computation.32 | loop fusion | bytes 17825792 | tf_op jit(solution)/shard_map/squeeze | solution.py:88
  106.7 5.2 slice.452
  111.9 7.9 %slice.456 = f32[1,16,32,2048]{3,0,2,1:T(1,128)} slice(f32[1,16,34,2048]{3,0,2,1:T(1,128)} %get-tuple-element.84), slice={[0:1], [0:16], [1:33], [0:2048]} | slice | bytes 8388608 | tf_op jit(solution)/shard_map/slice | solution.py:39
  119.8 11.4 %fusion.21 = f32[1,15,32,2048]{3,0,2,1:T(1,128)S(1)} fusion(f32[1,16,34,2048]{3,0,2,1:T(1,128)} %get-tuple-element.84, f32[1,16,34,2048]{3,0,2,1:T(1,128)S(1)} %get-tuple-element.83), kind=kLoop, calls=%fused_computation.59 | loop fusion | flops 3932160 | bytes 19660800 | tf_op jit(solution)/shard_map/mul | solution.py:48
  131.2 46.0 %copy_add_fusion = f32[1,16,32,2048]{3,0,2,1:T(1,128)S(1)} fusion(f32[1,16,32,2048]{3,2,1,0:T(8,128)S(1)} %copy-done.11, f32[1,15,32,2048]{3,0,2,1:T(1,128)S(1)} %fusion.21, f32[1,16,32,2048]{3,0,2,1:T(1,128)S(1)} %copy-done.15, f32[1,16,32,2048]{3,0,2,1:T(1,128)S(1)} %copy-done.13, f32[1,16,34,2048]{3,0,2,1:T(1,128)} %get-tuple-element.84, ...), kind=kLoop, calls=%fused_computation.52 | loop fusion | flops 24117248 | bytes 37486592 | tf_op jit(solution)/shard_map/add | solution.py:89
  183.5 88.4 %all-gather.3.cloned.1.call-done = f32[16,32,2048]{2,1,0:T(8,128)} async-done(((f32[2,32,2048]{2,1,0:T(8,128)}), f32[16,32,2048]{2,1,0:T(8,128)}) %all-gather.3.cloned.1.call-update) | async-done | bytes 4194320 | tf_op jit(solution)/shard_map/all_gather | solution.py:92
  271.9 6.8 %fusion.55 = f32[2,32,2048]{2,0,1:T(2,128)S(1)} fusion(f32[16,32,2048]{2,1,0:T(8,128)} %all-gather.3.cloned.1.call-done, pred[32,2048]{1,0:T(8,128)(4,1)S(1)} %get-tuple-element.99, f32[8,16,16]{2,1,0:T(8,128)S(1)} %copy-done, s32[]{:T(128)S(6)} %select_n.118), kind=kOutput, calls=%fused_computation.94 | convolution fusion | flops 25296896 | bytes 4785156 | tf_op jit(solution)/shard_map/ij,jxc->ixc/dot_general | solution.py:59
  293.1 5.1 fusion.133
  315.4 5.8 %collective-permute-start.2 = (f32[2,1,16,1,2048]{4,0,3,2,1:T(2,128)S(1)}, f32[2,1,16,1,2048]{4,0,3,2,1:T(2,128)S(1)}, u32[]{:S(2)}, u32[]{:S(2)}) collective-permute-start(f32[2,1,16,1,2048]{4,0,3,2,1:T(2,128)S(1)} %get-tuple-element.89), channel_id=1, source_target_pairs={{0,1},{1,2},{2,3},{3,4},{4,5},{5,6},{6,7},{7,8},{8,9},{9,10},{10,1... | collective-permute-start | bytes 786440 | tf_op jit(solution)/shard_map/ppermute | solution.py:23
  324.4 5.9 %collective-permute-done.3 = f32[2,1,16,1,2048]{4,0,3,2,1:T(2,128)S(1)} collective-permute-done((f32[2,1,16,1,2048]{4,0,3,2,1:T(2,128)S(1)}, f32[2,1,16,1,2048]{4,0,3,2,1:T(2,128)S(1)}, u32[]{:S(2)}, u32[]{:S(2)}) %collective-permute-start.3) | collective-permute-done | bytes 262176 | tf_op jit(solution)/shard_map/ppermute | solution.py:25
  330.3 8.1 %fusion.7 = f32[2,1,16,34,2048]{4,0,3,2,1:T(2,128)S(1)} fusion(f32[1,1,16,32,2048]{4,0,3,2,1:T(1,128)S(1)} %copy-done.8, f32[2,1,16,1,2048]{4,0,3,2,1:T(2,128)S(1)} %collective-permute-done.3, f32[1,1,16,32,2048]{4,0,3,2,1:T(1,128)S(1)} %bitcast.109, f32[2,1,16,1,2048]{4,0,3,2,1:T(2,128)S(1)} %collective-permute-done.2), kind=kLoop, calls=%fused_computation.25 | loop fusion | flops 6684672 | bytes 17825792 | tf_op jit(solution)/shard_map/concatenate | solution.py:21
  338.5 7.9 %slice_bitcast_fusion.1 = (f32[1,16,34,2048]{3,0,2,1:T(1,128)S(1)}, f32[1,16,34,2048]{3,0,2,1:T(1,128)}) fusion(f32[2,1,16,34,2048]{4,0,3,2,1:T(2,128)S(1)} %fusion.7), kind=kLoop, calls=%fused_computation.30 | loop fusion | bytes 17825792 | tf_op jit(solution)/shard_map/squeeze | solution.py:88
  346.4 5.2 slice.470
  351.5 7.9 %slice.474 = f32[1,16,32,2048]{3,0,2,1:T(1,128)} slice(f32[1,16,34,2048]{3,0,2,1:T(1,128)} %get-tuple-element.82), slice={[0:1], [0:16], [1:33], [0:2048]} | slice | bytes 8388608 | tf_op jit(solution)/shard_map/slice | solution.py:39
  359.4 11.4 %fusion.19 = f32[1,15,32,2048]{3,0,2,1:T(1,128)S(1)} fusion(f32[1,16,34,2048]{3,0,2,1:T(1,128)} %get-tuple-element.82, f32[1,16,34,2048]{3,0,2,1:T(1,128)S(1)} %get-tuple-element.81), kind=kLoop, calls=%fused_computation.55 | loop fusion | flops 3932160 | bytes 19660800 | tf_op jit(solution)/shard_map/mul | solution.py:48
  370.9 42.8 %multiply_add_fusion = f32[1,16,32,2048]{3,0,2,1:T(1,128)S(1)} fusion(f32[1,16,32,2048]{3,0,2,1:T(1,128)S(1)} %copy-done.6, f32[1,15,32,2048]{3,0,2,1:T(1,128)S(1)} %fusion.19, f32[1,16,32,2048]{3,0,2,1:T(1,128)S(1)} %copy-done.14, f32[1,16,32,2048]{3,0,2,1:T(1,128)S(1)} %copy-done.12, f32[1,16,34,2048]{3,0,2,1:T(1,128)} %get-tuple-element.82, ...), kind=kLoop, calls=%fused_computation.53 | loop fusion | flops 24117248 | bytes 37486592 | tf_op jit(solution)/shard_map/add | solution.py:89
  417.8 90.4 %all-gather.5.cloned.1.call-done = f32[16,32,2048]{2,1,0:T(8,128)} async-done(((f32[2,32,2048]{2,1,0:T(8,128)}), f32[16,32,2048]{2,1,0:T(8,128)}) %all-gather.5.cloned.1.call-update) | async-done | bytes 4194320 | tf_op jit(solution)/shard_map/all_gather | solution.py:92
  508.1 6.8 %fusion.79 = f32[2,32,2048]{2,0,1:T(2,128)S(1)} fusion(f32[16,32,2048]{2,1,0:T(8,128)} %all-gather.5.cloned.1.call-done, pred[32,2048]{1,0:T(8,128)(4,1)S(1)} %get-tuple-element.99, f32[8,16,16]{2,1,0:T(8,128)S(1)} %copy-done, s32[]{:T(128)S(6)} %select_n.118), kind=kOutput, calls=%fused_computation.102 | convolution fusion | flops 25296896 | bytes 4785156 | tf_op jit(solution)/shard_map/ij,jxc->ixc/dot_general | solution.py:59
  543.8 5.0 fusion.103
  (84 shorter events, 84.4 us)
Async XLA Ops:
  6.5 265.4 %copy-start = (f32[8,16,16]{2,1,0:T(8,128)S(1)}, f32[8,16,16]{2,1,0:T(8,128)}, u32[]{:S(2)}) copy-start(f32[8,16,16]{2,1,0:T(8,128)} %param.25) | copy-start | bytes 24580
  6.5 265.3 %all-gather.3.cloned.1.call-start = ((), (), s32[]{:S(2)}) async-start(), calls=%async_computation | async-start | bytes 4718592 | tf_op jit(solution)/shard_map/all_gather | solution.py:92
  58.3 32.5 %copy-start.7 = (f32[1,1,16,32,2048]{4,0,3,2,1:T(1,128)}, f32[1,1,16,32,2048]{4,0,3,2,1:T(1,128)S(1)}, u32[]{:S(2)}) copy-start(f32[1,1,16,32,2048]{4,0,3,2,1:T(1,128)S(1)} %fusion.8) | copy-start | bytes 12582916
  58.3 8.8 %copy-start.19 = (s32[1,32,2048]{2,1,0:T(8,128)S(1)}, s32[1,32,2048]{2,1,0:T(8,128)}, u32[]{:S(2)}) copy-start(s32[1,32,2048]{2,1,0:T(8,128)} %param.22) | copy-start | bytes 786436
  58.3 8.8 %copy-start.20 = (f32[1,128]{1,0:T(1,128)S(1)}, f32[1,128]{1,0:T(1,128)}, u32[]{:S(2)}) copy-start(f32[1,128]{1,0:T(1,128)} %param.24) | copy-start | bytes 1540
  58.9 31.9 %collective-permute-start = (f32[2,1,16,1,2048]{4,0,3,2,1:T(2,128)S(1)}, f32[2,1,16,1,2048]{4,0,3,2,1:T(2,128)S(1)}, u32[]{:S(2)}, u32[]{:S(2)}) collective-permute-start(f32[2,1,16,1,2048]{4,0,3,2,1:T(2,128)S(1)} %get-tuple-element.77), channel_id=1, source_target_pairs={{0,1},{1,2},{2,3},{3,4},{4,5},{5,6},{6,7},{7,8},{8,9},{9,10},{10,1... | collective-permute-start | bytes 786440 | tf_op jit(solution)/shard_map/ppermute | solution.py:23
  65.0 25.8 %collective-permute-start.1 = (f32[2,1,16,1,2048]{4,0,3,2,1:T(2,128)S(1)}, f32[2,1,16,1,2048]{4,0,3,2,1:T(2,128)S(1)}, u32[]{:S(2)}, u32[]{:S(2)}) collective-permute-start(f32[2,1,16,1,2048]{4,0,3,2,1:T(2,128)S(1)} %get-tuple-element.91), channel_id=1, source_target_pairs={{1,0},{2,1},{3,2},{4,3},{5,4},{6,5},{7,6},{8,7},{9,8},{10,9},{11,1... | collective-permute-start | bytes 786440 | tf_op jit(solution)/shard_map/ppermute | solution.py:25
  119.7 11.4 %copy-start.11 = (f32[1,16,32,2048]{3,2,1,0:T(8,128)S(1)}, f32[1,16,32,2048]{3,2,1,0:T(8,128)}, u32[]{:S(2)}) copy-start(f32[1,16,32,2048]{3,2,1,0:T(8,128)} %param.19) | copy-start | bytes 12582916
  119.7 11.4 %copy-start.13 = (f32[1,16,32,2048]{3,0,2,1:T(1,128)S(1)}, f32[1,16,32,2048]{3,0,2,1:T(1,128)}, u32[]{:S(2)}) copy-start(f32[1,16,32,2048]{3,0,2,1:T(1,128)} %slice.452) | copy-start | bytes 12582916
  119.7 11.4 %copy-start.15 = (f32[1,16,32,2048]{3,0,2,1:T(1,128)S(1)}, f32[1,16,32,2048]{3,0,2,1:T(1,128)}, u32[]{:S(2)}) copy-start(f32[1,16,32,2048]{3,0,2,1:T(1,128)} %slice.456) | copy-start | bytes 12582916
  177.2 5.2 copy-start.18
  177.2 5.9 %copy-start.17 = (s32[32,2048]{1,0:T(8,128)S(1)}, s32[32,2048]{1,0:T(8,128)}, u32[]{:S(2)}) copy-start(s32[32,2048]{1,0:T(8,128)} %param.21) | copy-start | bytes 786436
  181.3 326.8 %all-gather.5.cloned.1.call-start = ((), (), s32[]{:S(2)}) async-start(), calls=%async_computation.1 | async-start | bytes 4718592 | tf_op jit(solution)/shard_map/all_gather | solution.py:92
  271.9 6.8 %copy-start.1 = (f32[16,32,2048]{2,1,0:T(8,128)S(1)}, f32[16,32,2048]{2,1,0:T(8,128)}, u32[]{:S(2)}) copy-start(f32[16,32,2048]{2,1,0:T(8,128)} %all-gather.3.cloned.1.call-done) | copy-start | bytes 12582916
  303.0 9.7 %copy-start.4 = (f32[1,16,32,2048]{3,0,2,1:T(1,128)S(1)}, f32[1,16,32,2048]{3,0,2,1:T(1,128)}, u32[]{:S(2)}) copy-start(f32[1,16,32,2048]{3,0,2,1:T(1,128)} %copy-done.3) | copy-start | bytes 12582916
  312.6 17.7 %copy-start.8 = (f32[1,1,16,32,2048]{4,0,3,2,1:T(1,128)S(1)}, f32[1,1,16,32,2048]{4,0,3,2,1:T(1,128)}, u32[]{:S(2)}) copy-start(f32[1,1,16,32,2048]{4,0,3,2,1:T(1,128)} %copy-done.7) | copy-start | bytes 12582916
  315.0 31.4 %copy-start.5 = (f32[1,16,32,2048]{3,0,2,1:T(1,128)}, f32[1,16,32,2048]{3,0,2,1:T(1,128)S(1)}, u32[]{:S(2)}) copy-start(f32[1,16,32,2048]{3,0,2,1:T(1,128)S(1)} %fusion.147) | copy-start | bytes 12582916
  315.4 9.1 %collective-permute-start.2 = (f32[2,1,16,1,2048]{4,0,3,2,1:T(2,128)S(1)}, f32[2,1,16,1,2048]{4,0,3,2,1:T(2,128)S(1)}, u32[]{:S(2)}, u32[]{:S(2)}) collective-permute-start(f32[2,1,16,1,2048]{4,0,3,2,1:T(2,128)S(1)} %get-tuple-element.89), channel_id=1, source_target_pairs={{0,1},{1,2},{2,3},{3,4},{4,5},{5,6},{6,7},{7,8},{8,9},{9,10},{10,1... | collective-permute-start | bytes 786440 | tf_op jit(solution)/shard_map/ppermute | solution.py:23
  321.1 9.2 %collective-permute-start.3 = (f32[2,1,16,1,2048]{4,0,3,2,1:T(2,128)S(1)}, f32[2,1,16,1,2048]{4,0,3,2,1:T(2,128)S(1)}, u32[]{:S(2)}, u32[]{:S(2)}) collective-permute-start(f32[2,1,16,1,2048]{4,0,3,2,1:T(2,128)S(1)} %get-tuple-element.90), channel_id=1, source_target_pairs={{1,0},{2,1},{3,2},{4,3},{5,4},{6,5},{7,6},{8,7},{9,8},{10,9},{11,1... | collective-permute-start | bytes 786440 | tf_op jit(solution)/shard_map/ppermute | solution.py:25
  359.4 11.4 %copy-start.6 = (f32[1,16,32,2048]{3,0,2,1:T(1,128)S(1)}, f32[1,16,32,2048]{3,0,2,1:T(1,128)}, u32[]{:S(2)}) copy-start(f32[1,16,32,2048]{3,0,2,1:T(1,128)} %copy-done.5) | copy-start | bytes 12582916
  359.4 11.4 %copy-start.12 = (f32[1,16,32,2048]{3,0,2,1:T(1,128)S(1)}, f32[1,16,32,2048]{3,0,2,1:T(1,128)}, u32[]{:S(2)}) copy-start(f32[1,16,32,2048]{3,0,2,1:T(1,128)} %slice.470) | copy-start | bytes 12582916
  359.4 11.4 %copy-start.14 = (f32[1,16,32,2048]{3,0,2,1:T(1,128)S(1)}, f32[1,16,32,2048]{3,0,2,1:T(1,128)}, u32[]{:S(2)}) copy-start(f32[1,16,32,2048]{3,0,2,1:T(1,128)} %slice.474) | copy-start | bytes 12582916
  508.1 6.8 %copy-start.2 = (f32[16,32,2048]{2,1,0:T(8,128)S(1)}, f32[16,32,2048]{2,1,0:T(8,128)}, u32[]{:S(2)}) copy-start(f32[16,32,2048]{2,1,0:T(8,128)} %all-gather.5.cloned.1.call-done) | copy-start | bytes 12582916
  539.0 9.8 %copy-start.10 = (f32[1,16,32,2048]{3,0,2,1:T(1,128)S(1)}, f32[1,16,32,2048]{3,0,2,1:T(1,128)}, u32[]{:S(2)}) copy-start(f32[1,16,32,2048]{3,0,2,1:T(1,128)} %copy-done.9) | copy-start | bytes 12582916
  (3 other events, 9.0 us)
Sparse Core Ops, SparseCore 0:
  181.4 90.4 all-gather.2
  417.9 90.1 all-gather.4
where the time goes:
time: 567 us; the launch traced here: 562 us
  waiting for transfers between devices  186 us (33%)
  other arithmetic  180 us (32%)
  matrix products  105 us (19%)
  local copies, waits for them, and re-layouts  60.2 us (11%)
  starting transfers between devices  16.3 us (3%)
  between operations  14.2 us (3%)
    all_gather x2, waiting for transfers between devices, local(): gathered = lax.all_gather(planes, 'tier', axis=0, tiled=True)  179 us
    add x2, other arithmetic, local(): heating_snapshot = heating_snapshot + step_dt * conduct(padded_t, padded_k)  88.8 us
    dot_general x16, matrix products, select_solve(): jnp.einsum('ij,jxc->ixc', matrices[which], planes, precision=lax.Precisio...  81.2 us
    another operation x3, other arithmetic, local(): joined = padded(jnp.stack([heating_snapshot, kappa]), (('tile', 3),), 1)  45.7 us
    dot_general x1, matrix products, local(): jnp.dot(onehot.reshape(-1, POWER_TILES), dissipation_per_patch[0], precis...  23.6 us
    mul x2, other arithmetic, conduct(): 0.5 * (kcell[..., 1:, :, :] + kcell[..., :-1, :, :])  22.8 us
    concatenate x2, other arithmetic, padded(): jnp.concatenate([lax.ppermute(tail, axis, [(i, (i + 1) % count) for i in...  16.1 us
    slice x2, local copies, waits for them, and re-layouts, conduct(): centre = padded_t[..., 1:-1, :]  15.8 us
  transfers between devices with their start and end apart: 6, of which 4 were waited for; matrix products, arithmetic and copies ran while one was open for 5% of the time, Pallas kernels for 0%

commit v1 on v0

v1 whole, which is shorter than its diff:
```python
import functools

import jax
import jax.numpy as jnp
from jax import lax
from jax.experimental import pallas as pl
from jax.experimental.pallas import tpu as pltpu
from jax.sharding import PartitionSpec as P

STEPS = 2
STEP_DT = 0.04
MESH = pl.DeviceIdType.MESH
F32 = jnp.float32


def lookup(table, index):
    return jnp.take_along_axis(table, index, axis=1, mode="promise_in_bounds")


def heat_kernel(
    dims,
    t_hbm, lab_hbm, zone_hbm, patch_hbm, ktab, stab, mtab,
    out_hbm,
    t0, lab, t1, kk, t2, zone, patch, src, coef, planes, rx, part, solved, back,
    hs, hr, ks, kr,
    load_sem, out_sem, hs_sem, hr_sem, ks_sem, kr_sem,
    fs_sem, fr_sem, bs_sem, br_sem, own_sem,
):
    nt, nk, nl, nc, regions = dims
    per = nc // nt
    tiles = per * 4
    last = nl - 1
    me = lax.axis_index("tier")
    tile = lax.axis_index("tile")
    lane = lax.broadcasted_iota(jnp.int32, (8, 128), 1)
    sub = lax.broadcasted_iota(jnp.int32, (8, 128), 0)
    first_lane = lane == 0
    last_lane = lane == 127

    groups = ((0, 2), (nl - 2, nl), (2, nl - 2))
    for g, (a, b) in enumerate(groups):
        for c in range(nc):
            cols = pl.ds(128 * c, 128)
            pltpu.make_async_copy(t_hbm.at[0, pl.ds(a, b - a), :, cols], t0.at[pl.ds(a, b - a), c], load_sem.at[2 * g]).start()
            pltpu.make_async_copy(lab_hbm.at[0, pl.ds(a, b - a), :, cols], lab.at[pl.ds(a, b - a), c], load_sem.at[2 * g + 1]).start()
        if g == 1:
            for c in range(nc):
                cols = pl.ds(128 * c, 128)
                pltpu.make_async_copy(patch_hbm.at[0, :, cols], patch.at[c], load_sem.at[6]).start()
            for c in range(per):
                cols = pl.ds(pl.multiple_of((me * per + c) * 128, 128), 128)
                pltpu.make_async_copy(zone_hbm.at[:, cols], zone.at[c], load_sem.at[7]).start()

    def wait_load(g):
        a, b = groups[g]
        whole = pl.ds(a, b - a)
        pltpu.make_async_copy(t0.at[whole], t0.at[whole], load_sem.at[2 * g]).wait()
        pltpu.make_async_copy(lab.at[whole], lab.at[whole], load_sem.at[2 * g + 1]).wait()

    barrier = pltpu.get_barrier_semaphore()
    for d in range(1, nt):
        pl.semaphore_signal(barrier, inc=1, device_id={"tier": lax.rem(me + d, nt)}, device_id_type=MESH)

    @pl.when(tile > 0)
    def _():
        pl.semaphore_signal(barrier, inc=1, device_id={"tile": tile - 1}, device_id_type=MESH)

    @pl.when(tile < nk - 1)
    def _():
        pl.semaphore_signal(barrier, inc=1, device_id={"tile": tile + 1}, device_id_type=MESH)

    ktable = jnp.broadcast_to(ktab[...], (8, 128))
    stable = jnp.broadcast_to(stab[...], (8, 128))

    def fill_kappa(l):
        for c in range(nc):
            for q in range(4):
                kk[l, c, pl.ds(8 * q, 8), :] = lookup(ktable, lab[l, c, pl.ds(q, 8, stride=4), :])

    def edge_rows(ref, dst, where, l):
        for side, row in ((0, 0), (1, 31)):
            for c in range(0, nc, 8):
                n = min(8, nc - c)
                dst[where + (side, pl.ds(l * nc + c, n), slice(None))] = ref[l, pl.ds(c, n), row, :]

    def halo_copy(send, recv, ssem, rsem, at, sem_at, side, rows):
        return pltpu.make_async_remote_copy(
            src_ref=send.at[at + (side, rows)],
            dst_ref=recv.at[at + (side, rows)],
            send_sem=ssem.at[sem_at + (side,)],
            recv_sem=rsem.at[sem_at + (side,)],
            device_id={"tile": tile - 1 if side == 0 else tile + 1},
            device_id_type=MESH,
        )

    spans = (pl.ds(0, nc), pl.ds(last * nc, nc), pl.ds(nc, (nl - 2) * nc))

    def halos(step, what, start):
        copies = [(hs, hr, hs_sem, hr_sem, (step,), (step, what))]
        if step == 0:
            copies.append((ks, kr, ks_sem, kr_sem, (), (what,)))
        for side in (0, 1):
            sends = (tile > 0) if side == 0 else (tile < nk - 1)
            gets = (tile < nk - 1) if side == 0 else (tile > 0)
            for parts in copies:
                copy = halo_copy(*parts, side, spans[what])
                if start == "start":
                    @pl.when(sends)
                    def _(copy=copy):
                        copy.start()
                elif start == "recv":
                    @pl.when(gets)
                    def _(copy=copy):
                        copy.wait_recv()
                else:
                    @pl.when(sends)
                    def _(copy=copy):
                        copy.wait_send()

    zero_rows = jnp.zeros((nl * nc, 128), F32)

    @pl.when(tile == nk - 1)
    def _():
        for step in range(STEPS):
            hr[step, 0] = zero_rows
        kr[0] = zero_rows

    @pl.when(tile == 0)
    def _():
        for step in range(STEPS):
            hr[step, 1] = zero_rows
        kr[1] = zero_rows

    def layer(step, l, up, down, emit):
        if step == 0:
            def temp(l, c, q):
                return t0[l, c, pl.ds(q, 8, stride=4), :]
        else:
            def temp(l, c, q):
                return t1[l, c, pl.ds(8 * q, 8), :]

        def cond(l, c, q):
            return kk[l, c, pl.ds(8 * q, 8), :]

        zero = jnp.zeros((8, 128), F32)
        t_next = [temp(l, 0, q) for q in range(4)]
        k_next = [cond(l, 0, q) for q in range(4)]
        before = None
        for c in range(nc):
            t, k = t_next, k_next
            if c + 1 < nc:
                t_next = [temp(l, c + 1, q) for q in range(4)]
                k_next = [cond(l, c + 1, q) for q in range(4)]
            else:
                t_next = k_next = [zero] * 4
            row = pl.ds(l * nc + c, 1)
            below_t = jnp.broadcast_to(hr[step, 0, row, :], (8, 128))
            above_t = jnp.broadcast_to(hr[step, 1, row, :], (8, 128))
            below_k = jnp.broadcast_to(kr[0, row, :], (8, 128))
            above_k = jnp.broadcast_to(kr[1, row, :], (8, 128))
            t_down = t[1:] + [jnp.where(sub == 7, below_t, pltpu.roll(t[0], 7, 0))]
            k_down = k[1:] + [jnp.where(sub == 7, below_k, pltpu.roll(k[0], 7, 0))]
            fy = [(k[q] + k_down[q]) * (t_down[q] - t[q]) for q in range(4)]
            over = jnp.where(sub == 0, (k[0] + above_k) * (t[0] - above_t), pltpu.roll(fy[3], 1, 0))
            fx = []
            for q in range(4):
                tr = pltpu.roll(jnp.where(first_lane, t_next[q], t[q]), 127, 1)
                krr = pltpu.roll(jnp.where(first_lane, k_next[q], k[q]), 127, 1)
                fx.append((k[q] + krr) * (tr - t[q]))
            for q in range(4):
                if c == 0:
                    left = jnp.where(first_lane, k[q] * t[q], pltpu.roll(fx[q], 1, 1))
                else:
                    left = pltpu.roll(jnp.where(last_lane, before[q], fx[q]), 1, 1)
                new = t[q] + (fx[q] - left) + (fy[q] - (over if q == 0 else fy[q - 1]))
                if down:
                    new = new + (k[q] + cond(l + 1, c, q)) * (temp(l + 1, c, q) - t[q])
                if up:
                    new = new - (k[q] + cond(l - 1, c, q)) * (t[q] - temp(l - 1, c, q))
                emit(c, q, new)
            before = fx

    def mine(n):
        return pl.ds(pl.multiple_of(n * per, per), per)

    def forward(step, h, d):
        peer = lax.rem(me + d, nt)
        return pltpu.make_async_remote_copy(
            src_ref=planes.at[step, h, mine(peer)],
            dst_ref=rx.at[step, h, me],
            send_sem=fs_sem.at[step, h, d],
            recv_sem=fr_sem.at[step, h, d],
            device_id={"tier": peer},
            device_id_type=MESH,
        )

    def forward_own(step, h):
        return pltpu.make_async_copy(planes.at[step, h, mine(me)], rx.at[step, h, me], own_sem.at[step, h])

    def landing(step, h):
        return t1.at[h * last] if step == 0 else back.at[h]

    def backward(step, h, d):
        peer = lax.rem(me + d, nt)
        return pltpu.make_async_remote_copy(
            src_ref=solved.at[step, h, peer],
            dst_ref=landing(step, h).at[mine(me)],
            send_sem=bs_sem.at[step, h, d],
            recv_sem=br_sem.at[step, h, d],
            device_id={"tier": peer},
            device_id_type=MESH,
        )

    def backward_own(step, h):
        return pltpu.make_async_copy(solved.at[step, h, me], landing(step, h).at[mine(me)], own_sem.at[step, 2 + h])

    order = [d for d in range(1, nt)]

    def boundary(step, h):
        def emit(c, q, new):
            if h == 0:
                new = new + src[c, pl.ds(8 * q, 8), :]
            planes[step, h, c, pl.ds(8 * q, 8), :] = new
        layer(step, h * last, h == 1, h == 0, emit)
        for d in order:
            forward(step, h, d).start()
        forward_own(step, h).start()

    def solve(step):
        for h in (0, 1):
            forward_own(step, h).wait()
            for d in order:
                forward(step, h, d).wait_recv()
            for u in range(tiles):
                p = [rx[step, h, t, u // 4, pl.ds(8 * (u % 4), 8), :] for t in range(nt)]

                @pl.loop(0, 2 * nt)
                def _(i, p=p, u=u):
                    total = coef[i, h, 0, u] * p[0]
                    for t in range(1, nt):
                        total = total + coef[i, h, t, u] * p[t]
                    if h == 0:
                        part[i, u] = total
                    else:
                        solved[step, lax.rem(i, 2), i // 2, u // 4, pl.ds(8 * (u % 4), 8), :] = part[i, u] + total
        for h in (0, 1):
            for d in order:
                backward(step, h, d).start()
            backward_own(step, h).start()

    wait_load(0)
    wait_load(1)
    for l in (0, last):
        fill_kappa(l)
        edge_rows(t0, hs, (0,), l)
        edge_rows(kk, ks, (), l)
    greeted = (nt - 1) + (tile > 0).astype(jnp.int32) + (tile < nk - 1).astype(jnp.int32)
    pl.semaphore_wait(barrier, greeted)
    halos(0, 0, "start")
    halos(0, 1, "start")
    fill_kappa(1)
    fill_kappa(last - 1)
    pltpu.make_async_copy(patch, patch, load_sem.at[6]).wait()
    for c in range(nc):
        for q in range(4):
            src[c, pl.ds(8 * q, 8), :] = lookup(stable, patch[c, pl.ds(q, 8, stride=4), :])
    halos(0, 0, "recv")
    boundary(0, 0)
    halos(0, 1, "recv")
    boundary(0, 1)

    wait_load(2)

    @pl.loop(1, last)
    def _(l):
        fill_kappa(l)
        edge_rows(t0, hs, (0,), l)
        edge_rows(kk, ks, (), l)

    halos(0, 2, "start")

    pltpu.make_async_copy(zone, zone, load_sem.at[7]).wait()
    zones = [zone[u // 4, pl.ds(u % 4, 8, stride=4), :] for u in range(tiles)]

    @pl.loop(0, 2 * nt)
    def _(i):
        table = jnp.broadcast_to(mtab[pl.ds(i, 1), :], (8, 128))
        for t in range(nt):
            for h in (0, 1):
                for u in range(tiles):
                    coef[i, h, t, u] = lookup(table, zones[u] + (2 * t + h) * regions)

    halos(0, 2, "recv")

    def inner(step, l, dst):
        def emit(c, q, new):
            if step == 0:
                dst[l, c, pl.ds(8 * q, 8), :] = new
            else:
                dst[l, c, pl.ds(q, 8, stride=4), :] = new
        layer(step, l, True, True, emit)

    @pl.loop(1, last)
    def _(l):
        inner(0, l, t1)
        edge_rows(t1, hs, (1,), l)

    halos(1, 2, "start")
    solve(0)

    halos(1, 2, "recv")

    @pl.loop(2, last - 1)
    def _(l):
        inner(1, l, t2)

    def put(a, n):
        whole = pl.ds(a, n)
        return [
            pltpu.make_async_copy(t2.at[whole, c], out_hbm.at[whole, :, pl.ds(128 * c, 128)], out_sem.at[a])
            for c in range(nc)
        ]

    for copy in put(2, nl - 4):
        copy.start()
    for h in (0, 1):
        backward_own(0, h).wait()
        for d in order:
            backward(0, h, d).wait_recv()
        edge_rows(t1, hs, (1,), h * last)
        halos(1, h, "start")
    for h in (0, 1):
        halos(1, h, "recv")
        boundary(1, h)
    for l in (1, last - 1):
        inner(1, l, t2)
        for copy in put(l, 1):
            copy.start()
    solve(1)
    for h in (0, 1):
        backward_own(1, h).wait()
        for d in order:
            backward(1, h, d).wait_recv()
        for c in range(nc):
            for q in range(4):
                t2[h * last, c, pl.ds(q, 8, stride=4), :] = back[h, c, pl.ds(8 * q, 8), :]
        for copy in put(h * last, 1):
            copy.start()

    for a, n in ((2, nl - 4), (1, 1), (last - 1, 1), (0, 1), (last, 1)):
        whole = pl.ds(a, n)
        pltpu.make_async_copy(t2.at[whole], t2.at[whole], out_sem.at[a]).wait()
    for step in range(STEPS):
        for h in (0, 1):
            for d in order:
                forward(step, h, d).wait_send()
                backward(step, h, d).wait_send()
        for what in range(3):
            halos(step, what, "send")


def make_local(mesh):
    nt, nk = mesh.shape["tier"], mesh.shape["tile"]

    def local(temperature, labels, zones, patches, kappa, power, operators):
        _, nl, rows, cols = temperature.shape
        nc = cols // 128
        regions, block, _ = operators.shape
        dims = (nt, nk, nl, nc, regions)
        per = nc // nt

        def row(x):
            return jnp.pad(x, ((0, 0), (0, 128 - x.shape[1])))

        ktab = row((STEP_DT * 0.5) * kappa[None, :])
        stab = row(STEP_DT * power)
        mtab = row(operators.transpose(1, 2, 0).reshape(block, block * regions))
        any_spec = pl.BlockSpec(memory_space=pl.ANY)
        vmem = pl.BlockSpec(memory_space=pltpu.VMEM)
        dma = pltpu.SemaphoreType.DMA
        out = pl.pallas_call(
            functools.partial(heat_kernel, dims),
            out_shape=jax.ShapeDtypeStruct((nl, rows, cols), F32),
            in_specs=[any_spec] * 4 + [vmem] * 3,
            out_specs=any_spec,
            scratch_shapes=[
                pltpu.VMEM((nl, nc, 32, 128), F32),
                pltpu.VMEM((nl, nc, 32, 128), jnp.int32),
                pltpu.VMEM((nl, nc, 32, 128), F32),
                pltpu.VMEM((nl, nc, 32, 128), F32),
                pltpu.VMEM((nl, nc, 32, 128), F32),
                pltpu.VMEM((per, 32, 128), jnp.int32),
                pltpu.VMEM((nc, 32, 128), jnp.int32),
                pltpu.VMEM((nc, 32, 128), F32),
                pltpu.VMEM((2 * nt, 2, nt, per * 4, 8, 128), F32),
                pltpu.VMEM((STEPS, 2, nc, 32, 128), F32),
                pltpu.VMEM((STEPS, 2, nt, per, 32, 128), F32),
                pltpu.VMEM((2 * nt, per * 4, 8, 128), F32),
                pltpu.VMEM((STEPS, 2, nt, per, 32, 128), F32),
                pltpu.VMEM((2, nc, 32, 128), F32),
                pltpu.VMEM((STEPS, 2, nl * nc, 128), F32),
                pltpu.VMEM((STEPS, 2, nl * nc, 128), F32),
                pltpu.VMEM((2, nl * nc, 128), F32),
                pltpu.VMEM((2, nl * nc, 128), F32),
                dma((8,)),
                dma((nl,)),
                dma((STEPS, 3, 2)),
                dma((STEPS, 3, 2)),
                dma((3, 2)),
                dma((3, 2)),
                dma((STEPS, 2, nt)),
                dma((STEPS, 2, nt)),
                dma((STEPS, 2, nt)),
                dma((STEPS, 2, nt)),
                dma((STEPS, 4)),
            ],
            compiler_params=pltpu.CompilerParams(
                collective_id=0, has_side_effects=True, vmem_limit_bytes=56 * 1024 * 1024
            ),
            name="heat",
        )(temperature, labels, zones, patches, ktab, stab, mtab)
        return out[None]

    return local


def solution(mesh):
    in_specs = (
        P("tier", None, "tile", None),
        P("tier", None, "tile", None),
        P("tile", None),
        P("tier", "tile", None),
        P(),
        P("tier", None),
        P(),
    )
    out_specs = P("tier", None, "tile", None)
    return jax.shard_map(make_local(mesh), mesh=mesh, in_specs=in_specs, out_specs=out_specs, check_vma=False)
```

time: 567 us -> 77.8 us (0.14)
  the two profiles are of different devices: /device:TPU:7 before, /device:TPU:1 now
where the time goes in v1:
time: 77.8 us; the launch traced here: 77.6 us
  Pallas kernels  68.9 us (89%)
  local copies, waits for them, and re-layouts  6.82 us (9%)
  other arithmetic  1.85 us (2%)
    pallas_call x1, Pallas kernels, local(): pl.pallas_call(functools.partial(heat_kernel, dims), out_shape=jax.ShapeD...  68.9 us
    unnamed x1, local copies, waits for them, and re-layouts  4.7 us

profile of v1, /device:TPU:1, one launch (start us, length us, event | category | flops | bytes accessed | tf_op | source)
XLA Modules:
  0.0 77.6 jit_solution(7502308014554438770)
XLA Ops:
  0.0 0.7 multiply_bitcast_fusion
  0.7 0.5 pad.4.ktab
  1.2 1.2 %broadcast_multiply_fusion.stab = f32[1,128]{1,0:T(1,128)} fusion(f32[1,128]{1,0:T(1,128)} %param.12), kind=kLoop, calls=%fused_computation.1 | loop fusion | flops 128 | bytes 1024 | tf_op jit(solution)/shard_map/mul | solution.py:376
  2.4 0.9 %copy.9 = f32[16,16,8]{0,2,1:T(8,128)S(1)} copy(f32[16,16,8]{1,0,2:T(8,128)} %bitcast.7) | data formatting | bytes 16384 | tf_op jit(solution)/shard_map/transpose | solution.py:377
  3.3 0.7 copy.10.mtab
  4.0 68.9 %heat.1 = f32[16,32,2048]{2,1,0:T(8,128)} custom-call(f32[1,16,32,2048]{3,2,1,0:T(8,128)} %t_hbm.1, s32[1,16,32,2048]{3,2,1,0:T(8,128)} %lab_hbm.1, s32[32,2048]{1,0:T(8,128)} %zone_hbm.1, s32[1,32,2048]{2,1,0:T(8,128)} %patch_hbm.1, f32[1,128]{1,0:T(1,128)} %pad.4.ktab, f32[1,128]{1,0:T(1,128)} %broadcast_multiply_fusion.stab, f32[16,128]{1,0:T(8,128)} %copy.10.mtab), custom_call_target="tpu_custom_call" | custom-call | tf_op jit(solution)/shard_map/heat/pallas_call | solution.py:381
  72.9 4.7 %copy.12 = f32[1,16,32,2048]{3,2,1,0:T(8,128)} copy(f32[1,16,32,2048]{3,2,1,0:T(8,128)} %bitcast.5) | data formatting | bytes 8388608

commit v2 on v1

--- a/solution.py
+++ b/solution.py
@@ -14,16 +14,25 @@
 
 
 def lookup(table, index):
-    return jnp.take_along_axis(table, index, axis=1, mode="promise_in_bounds")
+    return lax.gather(
+        table,
+        index[..., None],
+        lax.GatherDimensionNumbers(
+            offset_dims=(), collapsed_slice_dims=(1,), start_index_map=(1,),
+            operand_batching_dims=(0,), start_indices_batching_dims=(0,),
+        ),
+        slice_sizes=(1, 1),
+        mode=lax.GatherScatterMode.PROMISE_IN_BOUNDS,
+    )
 
 
 def heat_kernel(
     dims,
-    t_hbm, lab_hbm, zone_hbm, patch_hbm, ktab, stab, mtab,
-    out_hbm,
-    t0, lab, t1, kk, t2, zone, patch, src, coef, planes, rx, part, solved, back,
-    hs, hr, ks, kr,
-    load_sem, out_sem, hs_sem, hr_sem, ks_sem, kr_sem,
+    t_hbm, lab_hbm, zone_hbm, patch_hbm, kappa, power, operators,
+    t2,
+    t0, lab, t1, kk, zone, patch, src, coef, planes, rx, part, solved, back,
+    hs, hr, ks, kr, ktab, mtab,
+    load_sem, hs_sem, hr_sem, ks_sem, kr_sem,
     fs_sem, fr_sem, bs_sem, br_sem, own_sem,
 ):
     nt, nk, nl, nc, regions = dims
@@ -69,8 +78,13 @@
     def _():
         pl.semaphore_signal(barrier, inc=1, device_id={"tile": tile + 1}, device_id_type=MESH)
 
-    ktable = jnp.broadcast_to(ktab[...], (8, 128))
-    stable = jnp.broadcast_to(stab[...], (8, 128))
+    ktab[...] = jnp.zeros((8, 128), F32)
+    ktab[:, 0:kappa.shape[1]] = jnp.broadcast_to((STEP_DT * 0.5) * kappa[...], (8, kappa.shape[1]))
+    ktable = ktab[...]
+    stable = jnp.broadcast_to(STEP_DT * power[...], (8, 128))
+    block = 2 * nt
+    for w in range(regions):
+        mtab[:, w * block:(w + 1) * block] = operators[w]
 
     def fill_kappa(l):
         for c in range(nc):
@@ -231,18 +245,20 @@
             forward_own(step, h).wait()
             for d in order:
                 forward(step, h, d).wait_recv()
-            for u in range(tiles):
-                p = [rx[step, h, t, u // 4, pl.ds(8 * (u % 4), 8), :] for t in range(nt)]
-
-                @pl.loop(0, 2 * nt)
-                def _(i, p=p, u=u):
-                    total = coef[i, h, 0, u] * p[0]
-                    for t in range(1, nt):
-                        total = total + coef[i, h, t, u] * p[t]
+            @pl.loop(0, tiles)
+            def _(u):
+                where = (u // 4, pl.ds(pl.multiple_of(8 * lax.rem(u, 4), 8), 8), slice(None))
+                p = [rx[(step, h, t) + where] for t in range(nt)]
+                for i in range(block):
+                    terms = [coef[i, h, t, u] * p[t] for t in range(nt)]
+                    if h == 1:
+                        terms.append(part[i, u])
+                    while len(terms) > 1:
+                        terms = [a + b for a, b in zip(terms[::2], terms[1::2])] + terms[len(terms) & ~1:]
                     if h == 0:
-                        part[i, u] = total
+                        part[i, u] = terms[0]
                     else:
-                        solved[step, lax.rem(i, 2), i // 2, u // 4, pl.ds(8 * (u % 4), 8), :] = part[i, u] + total
+                        solved[(step, i % 2, i // 2) + where] = terms[0]
         for h in (0, 1):
             for d in order:
                 backward(step, h, d).start()
@@ -280,7 +296,7 @@
     halos(0, 2, "start")
 
     pltpu.make_async_copy(zone, zone, load_sem.at[7]).wait()
-    zones = [zone[u // 4, pl.ds(u % 4, 8, stride=4), :] for u in range(tiles)]
+    zones = [zone[u // 4, pl.ds(u % 4, 8, stride=4), :] * block for u in range(tiles)]
 
     @pl.loop(0, 2 * nt)
     def _(i):
@@ -288,8 +304,9 @@
         for t in range(nt):
             for h in (0, 1):
                 for u in range(tiles):
-                    coef[i, h, t, u] = lookup(table, zones[u] + (2 * t + h) * regions)
-
+                    coef[i, h, t, u] = lookup(table, zones[u] + (2 * t + h))
+
+    solve(0)
     halos(0, 2, "recv")
 
     def inner(step, l, dst):
@@ -306,23 +323,7 @@
         edge_rows(t1, hs, (1,), l)
 
     halos(1, 2, "start")
-    solve(0)
-
-    halos(1, 2, "recv")
-
-    @pl.loop(2, last - 1)
-    def _(l):
-        inner(1, l, t2)
-
-    def put(a, n):
-        whole = pl.ds(a, n)
-        return [
-            pltpu.make_async_copy(t2.at[whole, c], out_hbm.at[whole, :, pl.ds(128 * c, 128)], out_sem.at[a])
-            for c in range(nc)
-        ]
-
-    for copy in put(2, nl - 4):
-        copy.start()
+
     for h in (0, 1):
         backward_own(0, h).wait()
         for d in order:
@@ -332,11 +333,15 @@
     for h in (0, 1):
         halos(1, h, "recv")
         boundary(1, h)
+    halos(1, 2, "recv")
+
+    @pl.loop(2, last - 1)
+    def _(l):
+        inner(1, l, t2)
+
+    solve(1)
     for l in (1, last - 1):
         inner(1, l, t2)
-        for copy in put(l, 1):
-            copy.start()
-    solve(1)
     for h in (0, 1):
         backward_own(1, h).wait()
         for d in order:
@@ -344,12 +349,7 @@
         for c in range(nc):
             for q in range(4):
                 t2[h * last, c, pl.ds(q, 8, stride=4), :] = back[h, c, pl.ds(8 * q, 8), :]
-        for copy in put(h * last, 1):
-            copy.start()
-
-    for a, n in ((2, nl - 4), (1, 1), (last - 1, 1), (0, 1), (last, 1)):
-        whole = pl.ds(a, n)
-        pltpu.make_async_copy(t2.at[whole], t2.at[whole], out_sem.at[a]).wait()
+
     for step in range(STEPS):
         for h in (0, 1):
             for d in order:
@@ -359,6 +359,16 @@
             halos(step, what, "send")
 
 
+def put_kernel(source, out, sem):
+    copies = [
+        pltpu.make_async_copy(source.at[:, c], out.at[:, :, pl.ds(128 * c, 128)], sem)
+        for c in range(source.shape[1])
+    ]
+    for copy in copies:
+        copy.start()
+    pltpu.make_async_copy(source, source, sem).wait()
+
+
 def make_local(mesh):
     nt, nk = mesh.shape["tier"], mesh.shape["tile"]
 
@@ -369,24 +379,17 @@
         dims = (nt, nk, nl, nc, regions)
         per = nc // nt
 
-        def row(x):
-            return jnp.pad(x, ((0, 0), (0, 128 - x.shape[1])))
-
-        ktab = row((STEP_DT * 0.5) * kappa[None, :])
-        stab = row(STEP_DT * power)
-        mtab = row(operators.transpose(1, 2, 0).reshape(block, block * regions))
         any_spec = pl.BlockSpec(memory_space=pl.ANY)
         vmem = pl.BlockSpec(memory_space=pltpu.VMEM)
         dma = pltpu.SemaphoreType.DMA
         out = pl.pallas_call(
             functools.partial(heat_kernel, dims),
-            out_shape=jax.ShapeDtypeStruct((nl, rows, cols), F32),
+            out_shape=pltpu.VMEM((nl, nc, 32, 128), F32),
             in_specs=[any_spec] * 4 + [vmem] * 3,
-            out_specs=any_spec,
+            out_specs=vmem,
             scratch_shapes=[
                 pltpu.VMEM((nl, nc, 32, 128), F32),
                 pltpu.VMEM((nl, nc, 32, 128), jnp.int32),
-                pltpu.VMEM((nl, nc, 32, 128), F32),
                 pltpu.VMEM((nl, nc, 32, 128), F32),
                 pltpu.VMEM((nl, nc, 32, 128), F32),
                 pltpu.VMEM((per, 32, 128), jnp.int32),
@@ -402,8 +405,9 @@
                 pltpu.VMEM((STEPS, 2, nl * nc, 128), F32),
                 pltpu.VMEM((2, nl * nc, 128), F32),
                 pltpu.VMEM((2, nl * nc, 128), F32),
+                pltpu.VMEM((8, 128), F32),
+                pltpu.VMEM((block, 128), F32),
                 dma((8,)),
-                dma((nl,)),
                 dma((STEPS, 3, 2)),
                 dma((STEPS, 3, 2)),
                 dma((3, 2)),
@@ -415,10 +419,19 @@
                 dma((STEPS, 4)),
             ],
             compiler_params=pltpu.CompilerParams(
-                collective_id=0, has_side_effects=True, vmem_limit_bytes=56 * 1024 * 1024
+                collective_id=0, has_side_effects=True, vmem_limit_bytes=62_800_000
             ),
             name="heat",
-        )(temperature, labels, zones, patches, ktab, stab, mtab)
+        )(temperature, labels, zones, patches, kappa[None], power, operators)
+        out = pl.pallas_call(
+            put_kernel,
+            out_shape=jax.ShapeDtypeStruct((nl, rows, cols), F32),
+            in_specs=[any_spec],
+            out_specs=any_spec,
+            scratch_shapes=[dma],
+            compiler_params=pltpu.CompilerParams(vmem_limit_bytes=1024 * 1024),
+            name="put",
+        )(out)
         return out[None]
 
     return local

time: 77.8 us -> 60.1 us (0.77)
  the two profiles are of different devices: /device:TPU:1 before, /device:TPU:7 now
where the time goes in v2:
time: 60.1 us; the launch traced here: 59.9 us
  Pallas kernels  59.9 us (100%)
    pallas_call x1, Pallas kernels, local(): pl.pallas_call(functools.partial(heat_kernel, dims), out_shape=pltpu.VMEM...  57.9 us
    pallas_call x1, Pallas kernels, local(): pl.pallas_call(put_kernel, out_shape=jax.ShapeDtypeStruct((nl, rows, cols...  2 us

profile of v2, /device:TPU:7, one launch (start us, length us, event | category | flops | bytes accessed | tf_op | source)
XLA Modules:
  0.0 59.9 jit_solution(7832539470670023627)
XLA Ops:
  0.0 57.9 %heat.1.source = f32[16,16,32,128]{3,2,1,0:T(8,128)S(1)} custom-call(f32[1,16,32,2048]{3,2,1,0:T(8,128)} %t_hbm.1, s32[1,16,32,2048]{3,2,1,0:T(8,128)} %lab_hbm.1, s32[32,2048]{1,0:T(8,128)} %zone_hbm.1, s32[1,32,2048]{2,1,0:T(8,128)} %patch_hbm.1, f32[1,16]{1,0:T(1,128)} %bitcast.2, f32[1,128]{1,0:T(1,128)} %power.1, f32[8,16,16]{2,1,0:T(8,128)} %operators.1), custom_call_target="tpu_custom_call" | custom-call | tf_op jit(solution)/shard_map/heat/pallas_call | solution.py:385
  57.9 2.0 %put.1 = f32[16,32,2048]{2,1,0:T(8,128)} custom-call(f32[16,16,32,128]{3,2,1,0:T(8,128)S(1)} %heat.1.source), custom_call_target="tpu_custom_call" | custom-call | tf_op jit(solution)/shard_map/put/pallas_call | solution.py:426

commit v3 on v2

v3 whole, which is shorter than its diff:
```python
import functools

import jax
import jax.numpy as jnp
from jax import lax
from jax.experimental import pallas as pl
from jax.experimental.pallas import tpu as pltpu
from jax.sharding import PartitionSpec as P

STEPS = 2
GROUP = (0, 2, 3, 1)
STEP_DT = 0.04
MESH = pl.DeviceIdType.MESH
F32 = jnp.float32


def group(q):
    return pl.ds(8 * GROUP[q], 8)


def lookup(table, index):
    return lax.gather(
        table,
        index[..., None],
        lax.GatherDimensionNumbers(
            offset_dims=(), collapsed_slice_dims=(1,), start_index_map=(1,),
            operand_batching_dims=(0,), start_indices_batching_dims=(0,),
        ),
        slice_sizes=(1, 1),
        mode=lax.GatherScatterMode.PROMISE_IN_BOUNDS,
    )


def heat_kernel(
    dims,
    t_hbm, lab_hbm, zone_hbm, patch_hbm, kappa_hbm, power_hbm, operators_hbm,
    t2,
    t0, lab, t1, kk, zone, patch, src, coef, planes, rx, solved,
    hs, hr, ks, kr, ls, lr, ktab, mtab, em, pe, re, he, ha, back, kappa, power, operators,
    load_sem, table_sem, hs_sem, hr_sem, ks_sem, kr_sem,
    fs_sem, fr_sem, bs_sem, br_sem, own_sem, es_sem, er_sem, as_sem, ar_sem,
):
    nt, nk, nl, nc, regions = dims
    per = nc // nt
    tiles = per * 4
    last = nl - 1
    me = lax.axis_index("tier")
    tile = lax.axis_index("tile")
    lane = lax.broadcasted_iota(jnp.int32, (8, 128), 1)
    sub = lax.broadcasted_iota(jnp.int32, (8, 128), 0)
    first_lane = lane == 0
    last_lane = lane == 127

    barrier = pltpu.get_barrier_semaphore()
    for d in range(1, nt):
        pl.semaphore_signal(barrier, inc=1, device_id={"tier": lax.rem(me + d, nt)}, device_id_type=MESH)

    @pl.when(tile > 0)
    def _():
        pl.semaphore_signal(barrier, inc=1, device_id={"tile": tile - 1}, device_id_type=MESH)

    @pl.when(tile < nk - 1)
    def _():
        pl.semaphore_signal(barrier, inc=1, device_id={"tile": tile + 1}, device_id_type=MESH)

    groups = ((0, 2), (nl - 2, nl), (2, nl - 2))

    def start_load(g):
        a, b = groups[g]
        for c in range(nc):
            cols = pl.ds(128 * c, 128)
            pltpu.make_async_copy(lab_hbm.at[0, pl.ds(a, b - a), :, cols], lab.at[pl.ds(a, b - a), c], load_sem.at[2 * g + 1]).start()
        for c in range(nc):
            cols = pl.ds(128 * c, 128)
            pltpu.make_async_copy(t_hbm.at[0, pl.ds(a, b - a), :, cols], t0.at[pl.ds(a, b - a), c], load_sem.at[2 * g]).start()

    def wait_load(g, labels):
        a, b = groups[g]
        whole = pl.ds(a, b - a)
        if labels:
            pltpu.make_async_copy(lab.at[whole], lab.at[whole], load_sem.at[2 * g + 1]).wait()
        else:
            pltpu.make_async_copy(t0.at[whole], t0.at[whole], load_sem.at[2 * g]).wait()

    tables = [
        pltpu.make_async_copy(kappa_hbm, kappa, table_sem.at[0]),
        pltpu.make_async_copy(power_hbm, power, table_sem.at[1]),
        pltpu.make_async_copy(operators_hbm, operators, table_sem.at[2]),
    ]
    for copy in tables:
        copy.start()
    start_load(0)
    for c in range(nc):
        cols = pl.ds(128 * c, 128)
        pltpu.make_async_copy(patch_hbm.at[0, :, cols], patch.at[c], load_sem.at[6]).start()
    start_load(1)
    for c in range(per):
        cols = pl.ds(pl.multiple_of((me * per + c) * 128, 128), 128)
        pltpu.make_async_copy(zone_hbm.at[:, cols], zone.at[c], load_sem.at[7]).start()
    start_load(2)

    for copy in tables:
        copy.wait()
    ktab[...] = jnp.zeros((8, 128), F32)
    ktab[:, 0:kappa.shape[1]] = jnp.broadcast_to((STEP_DT * 0.5) * kappa[...], (8, kappa.shape[1]))
    ktable = ktab[...]
    stable = jnp.broadcast_to(STEP_DT * power[...], (8, 128))
    block = 2 * nt
    for w in range(regions):
        mtab[:, w * block:(w + 1) * block] = operators[w]

    def fill_kappa(l):
        for c in range(nc):
            for q in range(4):
                kk[l, c, group(q), :] = lookup(ktable, lab[l, c, pl.ds(q, 8, stride=4), :])

    def edge_rows(ref, dst, where, l, far=15):
        for side, row in ((0, 0), (1, far)):
            for c in range(0, nc, 8):
                n = min(8, nc - c)
                dst[where + (side, pl.ds(l * nc + c, n), slice(None))] = ref[l, pl.ds(c, n), row, :]

    def halo_copy(send, recv, ssem, rsem, at, sem_at, side, rows):
        return pltpu.make_async_remote_copy(
            src_ref=send.at[at + (side, rows)],
            dst_ref=recv.at[at + (side, rows)],
            send_sem=ssem.at[sem_at + (side,)],
            recv_sem=rsem.at[sem_at + (side,)],
            device_id={"tile": tile - 1 if side == 0 else tile + 1},
            device_id_type=MESH,
        )

    cut = last // 2
    cut2 = cut + (last - 1 - cut) // 2
    spans = (
        pl.ds(0, nc), pl.ds(last * nc, nc),
        (pl.ds(nc, (nl - 2) * nc), pl.ds(nc, cut * nc)),
        (None, pl.ds((cut + 1) * nc, (last - 1 - cut) * nc)),
    )

    def halos(step, what, start):
        copies = [(hs, hr, hs_sem, hr_sem, (step,), (step, what))]
        if step == 0:
            copies.append((ls, lr, ks_sem, kr_sem, (), (what,)))
        rows = spans[what] if what < 2 else spans[what][step]
        for side in (0, 1):
            sends = (tile > 0) if side == 0 else (tile < nk - 1)
            gets = (tile < nk - 1) if side == 0 else (tile > 0)
            for parts in copies:
                copy = halo_copy(*parts, side, rows)
                if start == "start":
                    @pl.when(sends)
                    def _(copy=copy):
                        copy.start()
                elif start == "recv":
                    @pl.when(gets)
                    def _(copy=copy, labels=parts[1] is lr, side=side):
                        copy.wait_recv()
                        if labels:
                            first, count = rows.start // nc, rows.size // nc

                            @pl.loop(first, first + count)
                            def _(l):
                                for c in range(0, nc, 8):
                                    at = pl.ds(l * nc + c, min(8, nc - c))
                                    kr[side, at, :] = lookup(ktable[:min(8, nc - c)], lr[side, at, :])
                else:
                    @pl.when(sends)
                    def _(copy=copy):
                        copy.wait_send()

    def clear_outside():
        zero_rows = jnp.zeros((nl * nc, 128), F32)

        @pl.when(tile == nk - 1)
        def _():
            for step in range(STEPS):
                hr[step, 0] = zero_rows
            kr[0] = zero_rows
            ha[0] = jnp.zeros((8 * nt, 128), F32)

        @pl.when(tile == 0)
        def _():
            for step in range(STEPS):
                hr[step, 1] = zero_rows
            kr[1] = zero_rows
            ha[1] = jnp.zeros((8 * nt, 128), F32)

    def layer(step, l, up, down, outer, emit):
        if step == 0:
            def temp(l, c, q):
                return t0[l, c, pl.ds(q, 8, stride=4), :]
        else:
            def temp(l, c, q):
                return t1[l, c, group(q), :]

        def cond(l, c, q):
            return kk[l, c, group(q), :]

        zero = jnp.zeros((8, 128), F32)
        t_next = [temp(l, 0, q) for q in range(4)]
        k_next = [cond(l, 0, q) for q in range(4)]
        before = None
        for c in range(nc):
            t, k = t_next, k_next
            if c + 1 < nc:
                t_next = [temp(l, c + 1, q) for q in range(4)]
                k_next = [cond(l, c + 1, q) for q in range(4)]
            else:
                t_next = k_next = [zero] * 4
            if outer:
                row = pl.ds(l * nc + c, 1)
                below_t = jnp.broadcast_to(hr[step, 0, row, :], (8, 128))
                above_t = jnp.broadcast_to(hr[step, 1, row, :], (8, 128))
                below_k = jnp.broadcast_to(kr[0, row, :], (8, 128))
                above_k = jnp.broadcast_to(kr[1, row, :], (8, 128))
                k_down = k[1:] + [jnp.where(sub == 7, below_k, pltpu.roll(k[0], 7, 0))]
            else:
                below_t = t[3]
                k_down = k[1:] + [pltpu.roll(k[0], 7, 0)]
            t_down = t[1:] + [jnp.where(sub == 7, below_t, pltpu.roll(t[0], 7, 0))]
            fy = [(k[q] + k_down[q]) * (t_down[q] - t[q]) for q in range(4)]
            over = pltpu.roll(fy[3], 1, 0)
            if outer:
                over = jnp.where(sub == 0, (k[0] + above_k) * (t[0] - above_t), over)
            fx = []
            for q in range(4):
                tr = pltpu.roll(jnp.where(first_lane, t_next[q], t[q]), 127, 1)
                krr = pltpu.roll(jnp.where(first_lane, k_next[q], k[q]), 127, 1)
                fx.append((k[q] + krr) * (tr - t[q]))
            for q in range(4):
                if c == 0:
                    left = jnp.where(first_lane, k[q] * t[q], pltpu.roll(fx[q], 1, 1))
                else:
                    left = pltpu.roll(jnp.where(last_lane, before[q], fx[q]), 1, 1)
                new = t[q] + (fx[q] - left) + (fy[q] - (over if q == 0 else fy[q - 1]))
                if down:
                    new = new + (k[q] + cond(l + 1, c, q)) * (temp(l + 1, c, q) - t[q])
                if up:
                    new = new - (k[q] + cond(l - 1, c, q)) * (t[q] - temp(l - 1, c, q))
                emit(c, q, new)
            before = fx

    order = [d for d in range(1, nt)]
    chunks = [(h, part) for part in (1, 0) for h in (0, 1)]

    def half(part):
        return pl.ds(16 * part, 16)

    def columns(n):
        return pl.ds(pl.multiple_of(n * per, per), per)

    def forward(step, h, part, d):
        peer = lax.rem(me + d, nt)
        src_ref, dst_ref = planes.at[step, h, columns(peer), half(part)], rx.at[step, h, me, :, half(part)]
        if d == 0:
            return pltpu.make_async_copy(src_ref, dst_ref, own_sem.at[0, step, h, part])
        return pltpu.make_async_remote_copy(
            src_ref=src_ref,
            dst_ref=dst_ref,
            send_sem=fs_sem.at[step, h, part, d],
            recv_sem=fr_sem.at[step, h, part, d],
            device_id={"tier": peer},
            device_id_type=MESH,
        )

    def backward(step, h, part, d):
        peer = lax.rem(me + d, nt)
        landing = t1.at[h * last] if step == 0 else back.at[h]
        src_ref, dst_ref = solved.at[step, h, peer, :, half(part)], landing.at[columns(me), half(part)]
        if d == 0:
            return pltpu.make_async_copy(src_ref, dst_ref, own_sem.at[1, step, h, part])
        return pltpu.make_async_remote_copy(
            src_ref=src_ref,
            dst_ref=dst_ref,
            send_sem=bs_sem.at[step, h, part, d],
            recv_sem=br_sem.at[step, h, part, d],
            device_id={"tier": peer},
            device_id_type=MESH,
        )

    def edge_forward(step, d):
        peer = lax.rem(me + d, nt)
        rows = lambda n: pl.ds(pl.multiple_of(8 * n, 8), 8)
        src_ref, dst_ref = pe.at[step, rows(peer)], re.at[step, rows(me)]
        if d == 0:
            return pltpu.make_async_copy(src_ref, dst_ref, own_sem.at[2, step, 0, 0])
        return pltpu.make_async_remote_copy(
            src_ref=src_ref,
            dst_ref=dst_ref,
            send_sem=es_sem.at[step, d],
            recv_sem=er_sem.at[step, d],
            device_id={"tier": peer},
            device_id_type=MESH,
        )

    def edge_across(side, d):
        peer = lax.rem(me + d, nt)
        rows = lambda n: pl.ds(pl.multiple_of(8 * n, 8), 8)
        return pltpu.make_async_remote_copy(
            src_ref=he.at[rows(peer)],
            dst_ref=ha.at[side, rows(me)],
            send_sem=as_sem.at[side, d],
            recv_sem=ar_sem.at[side, d],
            device_id={"tier": peer, "tile": tile - 1 if side == 0 else tile + 1},
            device_id_type=MESH,
        )

    def edges_across(what):
        for side in (0, 1):
            sends = (tile > 0) if side == 0 else (tile < nk - 1)
            gets = (tile < nk - 1) if side == 0 else (tile > 0)

            @pl.when(gets if what == "recv" else sends)
            def _(side=side):
                for d in range(nt):
                    copy = edge_across(side, d)
                    if what == "start":
                        copy.start()
                    elif what == "recv":
                        copy.wait_recv()
                    else:
                        copy.wait_send()

    def boundary(step, h):
        def emit(c, q, new):
            if h == 0:
                new = new + src[c, group(q), :]
            planes[step, h, c, group(q), :] = new
        layer(step, h * last, h == 1, h == 0, False, emit)

    def send_planes(step):
        for h, part in chunks:
            for d in order + [0]:
                forward(step, h, part, d).start()

    def send_edges(step):
        for h in (0, 1):
            for side, row in ((0, 0), (1, 15)):
                for c in range(0, nc, 8):
                    n = min(8, nc - c)
                    em[h, side, pl.ds(c, n), :] = planes[step, h, pl.ds(c, n), row, :]
        for h in (0, 1):
            for side in (0, 1):
                for cc in range(per):
                    slot = (h * 2 + side) * per + cc
                    rows = pl.ds(h * last * nc + cc, nt, stride=per)
                    if step == 0:
                        th = hr[0, 1 - side, rows, :]
                    else:
                        th = ha[1 - side, pl.ds((h * 2 + 1 - side) * per + cc, nt, stride=8), :]
                    new = em[h, side, pl.ds(cc, nt, stride=per), :]
                    new = new + (ks[side, rows, :] + kr[1 - side, rows, :]) * (th - hs[step, side, rows, :])
                    pe[step, pl.ds(slot, nt, stride=8), :] = new
        for d in order + [0]:
            edge_forward(step, d).start()

    def solve(step, part):
        for h in (0, 1):
            forward(step, h, part, 0).wait()
            for d in order:
                forward(step, h, part, d).wait_recv()
        if part == 0:
            edge_forward(step, 0).wait()
            for d in order:
                edge_forward(step, d).wait_recv()
            for t in range(nt):
                for h in (0, 1):
                    for side, row in ((0, 0), (1, 15)):
                        for cc in range(per):
                            rx[step, h, t, cc, pl.ds(row, 1), :] = re[step, pl.ds(8 * t + (h * 2 + side) * per + cc, 1), :]

        @pl.loop(0, 2 * per)
        def _(n):
            rows = pl.ds(pl.multiple_of(16 * part + 8 * lax.rem(n, 2), 8), 8)
            cc = n // 2
            p = [rx[step, h, t, cc, rows, :] for h in (0, 1) for t in range(nt)]
            for i in range(block):
                terms = [coef[2 * per * part + n, i, j] * p[j] for j in range(block)]
                while len(terms) > 1:
                    terms = [a + b for a, b in zip(terms[::2], terms[1::2])]
                solved[step, i % 2, i // 2, cc, rows, :] = terms[0]

        for h in (0, 1):
            for d in order + [0]:
                backward(step, h, part, d).start()
        if part == 0 and step == 0:
            for t in range(nt):
                for h in (0, 1):
                    for side, row in ((0, 0), (1, 15)):
                        for cc in range(per):
                            he[pl.ds(8 * t + (h * 2 + side) * per + cc, 1), :] = solved[0, h, t, cc, pl.ds(row, 1), :]
            edges_across("start")

    def wait_back(step, part):
        for h in (0, 1):
            backward(step, h, part, 0).wait()
            for d in order:
                backward(step, h, part, d).wait_recv()

    def inner(step, l):
        def emit(c, q, new):
            if step == 0:
                t1[l, c, group(q), :] = new
            else:
                t2[l, c, pl.ds(q, 8, stride=4), :] = new
        layer(step, l, True, True, True, emit)
        if step == 0:
            edge_rows(t1, hs, (1,), l)

    def fill_coefficients(a, b):
        groups_of = [[0, 3], [1, 2]]
        zones = [
            zone[cc, pl.ds(q, 8, stride=4), :] * block
            for part in (0, 1) for cc in range(per) for q in groups_of[part]
        ]

        @pl.loop(a, b)
        def _(i):
            table = jnp.broadcast_to(mtab[pl.ds(i, 1), :], (8, 128))
            for u in range(tiles):
                for t in range(nt):
                    for h in (0, 1):
                        coef[u, i, h * nt + t] = lookup(table, zones[u] + (2 * t + h))

    wait_load(0, True)
    fill_kappa(0)
    fill_kappa(1)
    pltpu.make_async_copy(patch, patch, load_sem.at[6]).wait()
    for c in range(nc):
        for q in range(4):
            src[c, group(q), :] = lookup(stable, patch[c, pl.ds(q, 8, stride=4), :])
    wait_load(0, False)
    boundary(0, 0)
    wait_load(1, True)
    fill_kappa(last)
    fill_kappa(last - 1)
    wait_load(1, False)
    boundary(0, 1)
    for l in (0, last):
        edge_rows(t0, hs, (0,), l, 31)
        edge_rows(lab, ls, (), l, 31)
        edge_rows(kk, ks, (), l)
    pltpu.make_async_copy(zone, zone, load_sem.at[7]).wait()
    fill_coefficients(0, block // 4)
    wait_load(2, True)
    wait_load(2, False)

    @pl.loop(1, last)
    def _(l):
        edge_rows(t0, hs, (0,), l, 31)
        edge_rows(lab, ls, (), l, 31)

    greeted = (nt - 1) + (tile > 0).astype(jnp.int32) + (tile < nk - 1).astype(jnp.int32)
    pl.semaphore_wait(barrier, greeted)
    halos(0, 0, "start")
    halos(0, 1, "start")
    send_planes(0)
    halos(0, 2, "start")
    clear_outside()
    fill_coefficients(block // 4, block)
    halos(0, 0, "recv")
    halos(0, 1, "recv")
    send_edges(0)
    solve(0, 1)

    @pl.loop(2, last - 1)
    def _(l):
        fill_kappa(l)

    solve(0, 0)
    halos(0, 2, "recv")
    inner(0, last - 1)

    @pl.loop(1, cut + 1)
    def _(l):
        inner(0, l)

    halos(1, 2, "start")

    @pl.loop(cut + 1, cut2 + 1)
    def _(l):
        inner(0, l)

    wait_back(0, 1)
    wait_back(0, 0)
    for h in (0, 1):
        boundary(1, h)
    send_planes(1)
    for h in (0, 1):
        edge_rows(t1, hs, (1,), h * last)

    @pl.loop(cut2 + 1, last - 1)
    def _(l):
        inner(0, l)

    edges_across("recv")
    send_edges(1)
    halos(1, 3, "start")
    halos(1, 2, "recv")

    @pl.loop(2, cut + 1)
    def _(l):
        inner(1, l)

    solve(1, 1)
    inner(1, 1)
    solve(1, 0)
    halos(1, 3, "recv")

    @pl.loop(cut + 1, last)
    def _(l):
        inner(1, l)

    for part, qs in ((1, (1, 2)), (0, (0, 3))):
        wait_back(1, part)
        for h in (0, 1):
            for c in range(nc):
                for q in qs:
                    t2[h * last, c, pl.ds(q, 8, stride=4), :] = back[h, c, group(q), :]

    for step in range(STEPS):
        for h, part in chunks:
            for d in order:
                forward(step, h, part, d).wait_send()
                backward(step, h, part, d).wait_send()
        for d in order:
            edge_forward(step, d).wait_send()
    edges_across("send")
    for step, what in ((0, 0), (0, 1), (0, 2), (1, 2), (1, 3)):
        halos(step, what, "send")


def put_kernel(source, out, sem):
    copies = [
        pltpu.make_async_copy(source.at[:, c], out.at[:, :, pl.ds(128 * c, 128)], sem)
        for c in range(source.shape[1])
    ]
    for copy in copies:
        copy.start()
    pltpu.make_async_copy(source, source, sem).wait()


def make_local(mesh):
    nt, nk = mesh.shape["tier"], mesh.shape["tile"]

    def local(temperature, labels, zones, patches, kappa, power, operators):
        _, nl, rows, cols = temperature.shape
        nc = cols // 128
        regions, block, _ = operators.shape
        dims = (nt, nk, nl, nc, regions)
        per = nc // nt

        any_spec = pl.BlockSpec(memory_space=pl.ANY)
        vmem = pl.BlockSpec(memory_space=pltpu.VMEM)
        dma = pltpu.SemaphoreType.DMA
        out = pl.pallas_call(
            functools.partial(heat_kernel, dims),
            out_shape=pltpu.VMEM((nl, nc, 32, 128), F32),
            in_specs=[any_spec] * 7,
            out_specs=vmem,
            scratch_shapes=[
                pltpu.VMEM((nl, nc, 32, 128), F32),
                pltpu.VMEM((nl, nc, 32, 128), jnp.int32),
                pltpu.VMEM((nl, nc, 32, 128), F32),
                pltpu.VMEM((nl, nc, 32, 128), F32),
                pltpu.VMEM((per, 32, 128), jnp.int32),
                pltpu.VMEM((nc, 32, 128), jnp.int32),
                pltpu.VMEM((nc, 32, 128), F32),
                pltpu.VMEM((per * 4, block, block, 8, 128), F32),
                pltpu.VMEM((STEPS, 2, nc, 32, 128), F32),
                pltpu.VMEM((STEPS, 2, nt, per, 32, 128), F32),
                pltpu.VMEM((STEPS, 2, nt, per, 32, 128), F32),
                pltpu.VMEM((STEPS, 2, nl * nc, 128), F32),
                pltpu.VMEM((STEPS, 2, nl * nc, 128), F32),
                pltpu.VMEM((2, nl * nc, 128), F32),
                pltpu.VMEM((2, nl * nc, 128), F32),
                pltpu.VMEM((2, nl * nc, 128), jnp.int32),
                pltpu.VMEM((2, nl * nc, 128), jnp.int32),
                pltpu.VMEM((8, 128), F32),
                pltpu.VMEM((block, 128), F32),
                pltpu.VMEM((2, 2, nc, 128), F32),
                pltpu.VMEM((STEPS, 8 * nt, 128), F32),
                pltpu.VMEM((STEPS, 8 * nt, 128), F32),
                pltpu.VMEM((8 * nt, 128), F32),
                pltpu.VMEM((2, 8 * nt, 128), F32),
                pltpu.VMEM((2, nc, 32, 128), F32),
                pltpu.VMEM((1, kappa.shape[0]), F32),
                pltpu.VMEM((1, power.shape[1]), F32),
                pltpu.VMEM((regions, block, block), F32),
                dma((8,)),
                dma((3,)),
                dma((STEPS, 4, 2)),
                dma((STEPS, 4, 2)),
                dma((3, 2)),
                dma((3, 2)),
                dma((STEPS, 2, 2, nt)),
                dma((STEPS, 2, 2, nt)),
                dma((STEPS, 2, 2, nt)),
                dma((STEPS, 2, 2, nt)),
                dma((3, STEPS, 2, 2)),
                dma((STEPS, nt)),
                dma((STEPS, nt)),
                dma((2, nt)),
                dma((2, nt)),
            ],
            compiler_params=pltpu.CompilerParams(
                collective_id=0, has_side_effects=True, vmem_limit_bytes=62_800_000
            ),
            name="heat",
        )(temperature, labels, zones, patches, kappa[None], power, operators)
        out = pl.pallas_call(
            put_kernel,
            out_shape=jax.ShapeDtypeStruct((nl, rows, cols), F32),
            in_specs=[any_spec],
            out_specs=any_spec,
            scratch_shapes=[dma],
            compiler_params=pltpu.CompilerParams(vmem_limit_bytes=1024 * 1024),
            name="put",
        )(out)
        return out[None]

    return local


def solution(mesh):
    in_specs = (
        P("tier", None, "tile", None),
        P("tier", None, "tile", None),
        P("tile", None),
        P("tier", "tile", None),
        P(),
        P("tier", None),
        P(),
    )
    out_specs = P("tier", None, "tile", None)
    return jax.shard_map(make_local(mesh), mesh=mesh, in_specs=in_specs, out_specs=out_specs, check_vma=False)
```

time: 60.1 us -> 56.4 us (0.938)
  Pallas kernels: 59.9 us -> 55.9 us
    pallas_call x1, Pallas kernels: 57.9 us -> 53.9 us  [local(): pl.pallas_call(functools.partial(heat_kernel, dims), out_shape=pltpu.VMEM...]
where the time goes in v3:
time: 56.4 us; the launch traced here: 55.9 us
  Pallas kernels  55.9 us (99%)
    pallas_call x1, Pallas kernels, local(): pl.pallas_call(functools.partial(heat_kernel, dims), out_shape=pltpu.VMEM...  53.9 us
    pallas_call x1, Pallas kernels, local(): pl.pallas_call(put_kernel, out_shape=jax.ShapeDtypeStruct((nl, rows, cols...  2 us

profile of v3, /device:TPU:7, one launch (start us, length us, event | category | flops | bytes accessed | tf_op | source)
XLA Modules:
  0.0 55.9 jit_solution(2934140636876439835)
XLA Ops:
  0.0 53.9 %heat.1.source = f32[16,16,32,128]{3,2,1,0:T(8,128)S(1)} custom-call(f32[1,16,32,2048]{3,2,1,0:T(8,128)} %t_hbm.1, s32[1,16,32,2048]{3,2,1,0:T(8,128)} %lab_hbm.1, s32[32,2048]{1,0:T(8,128)} %zone_hbm.1, s32[1,32,2048]{2,1,0:T(8,128)} %patch_hbm.1, f32[1,16]{1,0:T(1,128)} %bitcast.2, f32[1,128]{1,0:T(1,128)} %power_hbm.1, f32[8,16,16]{2,1,0:T(8,128)} %operators_hbm.1), custom_call_target="tpu_custom_call" | custom-call | tf_op jit(solution)/shard_map/heat/pallas_call | solution.py:557
  53.9 2.0 %put.1 = f32[16,32,2048]{2,1,0:T(8,128)} custom-call(f32[16,16,32,128]{3,2,1,0:T(8,128)S(1)} %heat.1.source), custom_call_target="tpu_custom_call" | custom-call | tf_op jit(solution)/shard_map/put/pallas_call | solution.py:612

commit v4 on v3

--- a/solution.py
+++ b/solution.py
@@ -97,7 +97,6 @@
     for c in range(per):
         cols = pl.ds(pl.multiple_of((me * per + c) * 128, 128), 128)
         pltpu.make_async_copy(zone_hbm.at[:, cols], zone.at[c], load_sem.at[7]).start()
-    start_load(2)
 
     for copy in tables:
         copy.wait()
@@ -132,17 +131,22 @@
 
     cut = last // 2
     cut2 = cut + (last - 1 - cut) // 2
+    cut0 = (cut + 1) // 2
+
+    def layers(a, b):
+        return pl.ds(a * nc, (b - a) * nc)
+
+    ends = (layers(0, 1), layers(last, last + 1))
     spans = (
-        pl.ds(0, nc), pl.ds(last * nc, nc),
-        (pl.ds(nc, (nl - 2) * nc), pl.ds(nc, cut * nc)),
-        (None, pl.ds((cut + 1) * nc, (last - 1 - cut) * nc)),
+        ends + (layers(1, cut0 + 1), layers(cut0 + 1, cut + 1), layers(cut + 1, cut2 + 1), layers(cut2 + 1, last)),
+        ends + (layers(1, cut + 1), layers(cut + 1, last)),
     )
 
     def halos(step, what, start):
         copies = [(hs, hr, hs_sem, hr_sem, (step,), (step, what))]
         if step == 0:
             copies.append((ls, lr, ks_sem, kr_sem, (), (what,)))
-        rows = spans[what] if what < 2 else spans[what][step]
+        rows = spans[step][what]
         for side in (0, 1):
             sends = (tile > 0) if side == 0 else (tile < nk - 1)
             gets = (tile < nk - 1) if side == 0 else (tile > 0)
@@ -329,8 +333,8 @@
             planes[step, h, c, group(q), :] = new
         layer(step, h * last, h == 1, h == 0, False, emit)
 
-    def send_planes(step):
-        for h, part in chunks:
+    def send_planes(step, h):
+        for part in (1, 0):
             for d in order + [0]:
                 forward(step, h, part, d).start()
 
@@ -392,11 +396,10 @@
                             he[pl.ds(8 * t + (h * 2 + side) * per + cc, 1), :] = solved[0, h, t, cc, pl.ds(row, 1), :]
             edges_across("start")
 
-    def wait_back(step, part):
-        for h in (0, 1):
-            backward(step, h, part, 0).wait()
-            for d in order:
-                backward(step, h, part, d).wait_recv()
+    def wait_back(step, h, part):
+        backward(step, h, part, 0).wait()
+        for d in order:
+            backward(step, h, part, d).wait_recv()
 
     def inner(step, l):
         def emit(c, q, new):
@@ -433,16 +436,22 @@
     wait_load(0, False)
     boundary(0, 0)
     wait_load(1, True)
-    fill_kappa(last)
-    fill_kappa(last - 1)
     wait_load(1, False)
-    boundary(0, 1)
     for l in (0, last):
         edge_rows(t0, hs, (0,), l, 31)
         edge_rows(lab, ls, (), l, 31)
+    start_load(2)
+    greeted = (nt - 1) + (tile > 0).astype(jnp.int32) + (tile < nk - 1).astype(jnp.int32)
+    pl.semaphore_wait(barrier, greeted)
+    halos(0, 0, "start")
+    halos(0, 1, "start")
+    send_planes(0, 0)
+    fill_kappa(last)
+    fill_kappa(last - 1)
+    boundary(0, 1)
+    send_planes(0, 1)
+    for l in (0, last):
         edge_rows(kk, ks, (), l)
-    pltpu.make_async_copy(zone, zone, load_sem.at[7]).wait()
-    fill_coefficients(0, block // 4)
     wait_load(2, True)
     wait_load(2, False)
 
@@ -451,42 +460,45 @@
         edge_rows(t0, hs, (0,), l, 31)
         edge_rows(lab, ls, (), l, 31)
 
-    greeted = (nt - 1) + (tile > 0).astype(jnp.int32) + (tile < nk - 1).astype(jnp.int32)
-    pl.semaphore_wait(barrier, greeted)
-    halos(0, 0, "start")
-    halos(0, 1, "start")
-    send_planes(0)
     halos(0, 2, "start")
     clear_outside()
-    fill_coefficients(block // 4, block)
+    pltpu.make_async_copy(zone, zone, load_sem.at[7]).wait()
+    fill_coefficients(0, block // 2)
     halos(0, 0, "recv")
     halos(0, 1, "recv")
     send_edges(0)
+    halos(0, 3, "start")
+    fill_coefficients(block // 2, block)
     solve(0, 1)
+    halos(0, 5, "start")
 
     @pl.loop(2, last - 1)
     def _(l):
         fill_kappa(l)
 
     solve(0, 0)
+    halos(0, 4, "start")
     halos(0, 2, "recv")
-    inner(0, last - 1)
+    halos(0, 3, "recv")
 
     @pl.loop(1, cut + 1)
     def _(l):
         inner(0, l)
 
     halos(1, 2, "start")
+    halos(0, 5, "recv")
+    inner(0, last - 1)
+    halos(0, 4, "recv")
 
     @pl.loop(cut + 1, cut2 + 1)
     def _(l):
         inner(0, l)
 
-    wait_back(0, 1)
-    wait_back(0, 0)
     for h in (0, 1):
+        wait_back(0, h, 1)
+        wait_back(0, h, 0)
         boundary(1, h)
-    send_planes(1)
+        send_planes(1, h)
     for h in (0, 1):
         edge_rows(t1, hs, (1,), h * last)
 
@@ -513,8 +525,8 @@
         inner(1, l)
 
     for part, qs in ((1, (1, 2)), (0, (0, 3))):
-        wait_back(1, part)
         for h in (0, 1):
+            wait_back(1, h, part)
             for c in range(nc):
                 for q in qs:
                     t2[h * last, c, pl.ds(q, 8, stride=4), :] = back[h, c, group(q), :]
@@ -527,7 +539,7 @@
         for d in order:
             edge_forward(step, d).wait_send()
     edges_across("send")
-    for step, what in ((0, 0), (0, 1), (0, 2), (1, 2), (1, 3)):
+    for step, what in ((0, 0), (0, 1), (0, 2), (0, 3), (0, 4), (0, 5), (1, 2), (1, 3)):
         halos(step, what, "send")
 
 
@@ -590,10 +602,10 @@
                 pltpu.VMEM((regions, block, block), F32),
                 dma((8,)),
                 dma((3,)),
-                dma((STEPS, 4, 2)),
-                dma((STEPS, 4, 2)),
-                dma((3, 2)),
-                dma((3, 2)),
+                dma((STEPS, 6, 2)),
+                dma((STEPS, 6, 2)),
+                dma((6, 2)),
+                dma((6, 2)),
                 dma((STEPS, 2, 2, nt)),
                 dma((STEPS, 2, 2, nt)),
                 dma((STEPS, 2, 2, nt)),

time: 56.4 us -> 51.8 us (0.918)
  Pallas kernels: 55.9 us -> 51.6 us
    pallas_call x1, Pallas kernels: 53.9 us -> 49.6 us  [local(): pl.pallas_call(functools.partial(heat_kernel, dims), out_shape=pltpu.VMEM...]
where the time goes in v4:
time: 51.8 us; the launch traced here: 51.6 us
  Pallas kernels  51.6 us (100%)
    pallas_call x1, Pallas kernels, local(): pl.pallas_call(functools.partial(heat_kernel, dims), out_shape=pltpu.VMEM...  49.6 us
    pallas_call x1, Pallas kernels, local(): pl.pallas_call(put_kernel, out_shape=jax.ShapeDtypeStruct((nl, rows, cols...  2 us

profile of v4, /device:TPU:7, one launch (start us, length us, event | category | flops | bytes accessed | tf_op | source)
XLA Modules:
  0.0 51.6 jit_solution(2380435993125433868)
XLA Ops:
  0.0 49.6 %heat.1.source = f32[16,16,32,128]{3,2,1,0:T(8,128)S(1)} custom-call(f32[1,16,32,2048]{3,2,1,0:T(8,128)} %t_hbm.1, s32[1,16,32,2048]{3,2,1,0:T(8,128)} %lab_hbm.1, s32[32,2048]{1,0:T(8,128)} %zone_hbm.1, s32[1,32,2048]{2,1,0:T(8,128)} %patch_hbm.1, f32[1,16]{1,0:T(1,128)} %bitcast.2, f32[1,128]{1,0:T(1,128)} %power_hbm.1, f32[8,16,16]{2,1,0:T(8,128)} %operators_hbm.1), custom_call_target="tpu_custom_call" | custom-call | tf_op jit(solution)/shard_map/heat/pallas_call | solution.py:569
  49.6 2.0 %put.1 = f32[16,32,2048]{2,1,0:T(8,128)} custom-call(f32[16,16,32,128]{3,2,1,0:T(8,128)S(1)} %heat.1.source), custom_call_target="tpu_custom_call" | custom-call | tf_op jit(solution)/shard_map/put/pallas_call | solution.py:624
